TPU v7x, 32 devices: a whole 2x2x4 slice. The times are simulated.
32 devices in a mesh: ctx: 8 (over z, x), head: 4 (over y, core).
Axes of the slice: x: 2, y: 2, z: 4, core: 2. Of those that a mesh axis runs over, the one named last changes fastest.
Arguments:
- query: bfloat16 [8, 2, 128, 8192], P('ctx', None, 'head'), may hold values from -200 to 200
- keyval: bfloat16 [8, 2, 2, 128, 1024], P('ctx', None, None, 'head'), may hold values from -6 to 6
- doc_blocks: int32 [4], replicated, may hold values from 1 to 12, 16 in all
Outputs:
- attended: bfloat16 [8, 2, 128, 8192], P('ctx', None, 'head')
Inputs may be any that keep to these rules, and one draw needn't show every extreme that they name: `doc_blocks`: documents fill the sequence in order; the longest has exactly 12 blocks.
All inputs are finite; a program needn't handle non-finite values.
Results may differ from a plain program's by a relative error of at most 0.0038.
Values may be sent and summed in bfloat16 or wider, within the bound.
A program may use at most 64 MiB of HBM per device.

v0:
```python
import jax
import jax.numpy as jnp
from jax import lax
from jax.sharding import PartitionSpec as P

QUERY_HEADS = 64
KEY_VALUE_HEADS = 8
HEAD_WIDTH = 128
BLK = 128


def doc_index(positions, doc_ends):
    return jnp.sum((positions[:, None] >= doc_ends[None, :]).astype(jnp.int32), axis=1)


def local(query, keyval, doc_blocks):
    ctx_count = lax.axis_size("ctx")
    ctx_index = lax.axis_index("ctx")
    span_len = query.shape[2] * lax.axis_size("head")
    width_kv = keyval.shape[4]
    stacked = keyval.reshape(1, 4, keyval.shape[3], width_kv)
    query_heads, kv_heads = (
        lax.all_to_all(query, "head", split_axis=3, concat_axis=2, tiled=True),
        lax.all_to_all(stacked, "head", split_axis=3, concat_axis=2, tiled=True),
    )
    kv_local = kv_heads.shape[3] // HEAD_WIDTH
    heads_per_group = QUERY_HEADS // KEY_VALUE_HEADS
    kv_mine = kv_heads.reshape(1, 2, 2, span_len, kv_local * HEAD_WIDTH)
    row_count = 2 * span_len
    query_rows = query_heads.reshape(row_count, kv_local, heads_per_group, HEAD_WIDTH)
    offsets = jnp.arange(span_len, dtype=jnp.int32)
    query_pos = jnp.concatenate(
        [ctx_index * span_len + offsets, (2 * ctx_count - 1 - ctx_index) * span_len + offsets]
    )
    doc_ends = jnp.cumsum(doc_blocks) * BLK
    query_doc = doc_index(query_pos, doc_ends)
    scale_factor = HEAD_WIDTH ** (-0.5)
    initial = (
        jnp.full((kv_local, heads_per_group, row_count), -1e30, jnp.float32),
        jnp.zeros((kv_local, heads_per_group, row_count), jnp.float32),
        jnp.zeros((row_count, kv_local, heads_per_group, HEAD_WIDTH), jnp.float32),
    )
    gathered = lax.all_gather(kv_mine, "ctx", axis=0, tiled=True)
    running = initial
    count = gathered.shape[0]
    group_size = 4
    group_count = count // group_size
    grouped = gathered.reshape(group_count, group_size, 2, 2, span_len, kv_local * HEAD_WIDTH)
    firsts = jnp.arange(group_count, dtype=jnp.int32) * group_size

    def advance(state, payload):
        block_kv, lead_span = payload
        span_ids = lead_span + jnp.arange(group_size, dtype=jnp.int32)
        lower_pos = span_ids[:, None] * span_len + offsets[None, :]
        upper_pos = (2 * ctx_count - 1 - span_ids)[:, None] * span_len + offsets[None, :]
        key_pos = jnp.stack([lower_pos, upper_pos], axis=1).reshape(-1)
        key_row_block = block_kv[:, 0].reshape(-1, kv_local, HEAD_WIDTH)
        value_rows = block_kv[:, 1].reshape(-1, kv_local, HEAD_WIDTH)
        visible = (query_doc[:, None] == doc_index(key_pos, doc_ends)[None, :]) & (
            key_pos[None, :] <= query_pos[:, None]
        )
        row_max, totals, acc_sum = state
        scores = (
            jnp.einsum(
                "rgjd,kgd->gjrk", query_rows, key_row_block, preferred_element_type=jnp.float32
            )
            * scale_factor
        )
        scores = jnp.where(visible[None, None], scores, -1e30)
        new_max = jnp.maximum(row_max, jnp.max(scores, axis=-1))
        probs = jnp.where(visible[None, None], jnp.exp(scores - new_max[..., None]), 0.0)
        rescale = jnp.exp(row_max - new_max)
        totals = totals * rescale + jnp.sum(probs, axis=-1)
        added = jnp.einsum(
            "gjrk,kgd->rgjd",
            probs.astype(jnp.bfloat16),
            value_rows,
            preferred_element_type=jnp.float32,
        )
        acc_sum = acc_sum * jnp.moveaxis(rescale, 2, 0)[..., None] + added
        state = (new_max, totals, acc_sum)
        return (state, None)

    running, _ = lax.scan(advance, running, (grouped, firsts))
    row_max, totals, acc_sum = running
    result = (acc_sum / jnp.moveaxis(totals, 2, 0)[..., None]).astype(jnp.bfloat16)
    result = result.reshape(1, 2, span_len, kv_local * heads_per_group * HEAD_WIDTH)
    return lax.all_to_all(result, "head", split_axis=2, concat_axis=3, tiled=True)


def solution(mesh):
    placed = (P("ctx", None, "head", None), P("ctx", None, None, "head", None), P())
    return jax.shard_map(
        local, mesh=mesh, in_specs=placed, out_specs=P("ctx", None, "head", None), check_vma=False
    )
```

profile of v0, /device:TPU:1, one launch (start us, length us, event | category | flops | bytes accessed | tf_op | source)
XLA Modules:
  0.0 153.3 jit_solution(14284918072613798459)
XLA Ops:
  6.5 2.2 %copy.50 = bf16[1,2,2,32,1024]{3,2,1,4,0:T(2,128)(2,1)S(1)} copy(bf16[1,2,2,32,1024]{4,3,2,1,0:T(8,128)(2,1)} %param.6) | data formatting | bytes 524288 | tf_op args[1]
  8.8 1.0 reshape.201
  9.7 9.0 %all_to_all.48 = bf16[4,2,16384]{2,1,0:T(2,128)(2,1)S(1)} all-to-all(bf16[4,2,16384]{2,1,0:T(2,128)(2,1)S(1)} %reshape.201), channel_id=1, replica_groups=mesh['ctx'=8,'head'=4] {'head'}, dimensions={0} | all-to-all | bytes 524288 | tf_op jit(solution)/shard_map/all_to_all | solution.py:24
  18.8 0.5 reshape.202
  19.3 0.7 copy.64
  20.0 0.7 copy.52
  20.7 9.2 %copy.53 = bf16[1,2,32,8192]{2,1,0,3:T(2,128)(2,1)} copy(bf16[1,2,32,8192]{3,2,1,0:T(8,128)(2,1)} %param.5) | data formatting | bytes 2097152 | tf_op args[0]
  29.9 6.4 %reshape.203 = bf16[4,2,65536]{2,1,0:T(2,128)(2,1)} reshape(bf16[8192,1,2,32]{3,2,1,0:T(2,128)(2,1)} %bitcast.85) | data formatting | bytes 2097152
  36.3 4.5 %all-to-all-start.1 = ((bf16[4,2,65536]{2,1,0:T(2,128)(2,1)}), bf16[4,2,65536]{2,1,0:T(2,128)(2,1)S(1)}, u32[]{:S(2)}, u32[]{:S(2)}) async-start(bf16[4,2,65536]{2,1,0:T(2,128)(2,1)} %reshape.203), calls=%async_computation.1 | async-start | bytes 2097152 | tf_op jit(solution)/shard_map/all_to_all | solution.py:23
  40.8 0.2 reduce-window.7
  41.0 0.1 convert_reduce_fusion.1
  41.1 13.3 %all-to-all-done.1 = bf16[4,2,65536]{2,1,0:T(2,128)(2,1)S(1)} async-done(((bf16[4,2,65536]{2,1,0:T(2,128)(2,1)}), bf16[4,2,65536]{2,1,0:T(2,128)(2,1)S(1)}, u32[]{:S(2)}, u32[]{:S(2)}) %all-to-all-start.1) | async-done | bytes 1048608 | tf_op jit(solution)/shard_map/all_to_all | solution.py:23
  54.4 3.5 %reshape.204 = bf16[8192,1,2,32]{3,2,1,0:T(2,128)(2,1)} reshape(bf16[4,2,65536]{2,1,0:T(2,128)(2,1)S(1)} %all-to-all-done.1) | data formatting | bytes 2097152
  57.9 9.0 %copy.54 = bf16[1,2,32,4,2048]{4,2,3,1,0:T(8,128)(2,1)S(1)} copy(bf16[1,2,32,4,2048]{2,1,4,3,0:T(2,128)(2,1)} %bitcast.84) | data formatting | bytes 2097152 | tf_op jit(solution)/shard_map/all_to_all | solution.py:23
  66.9 0.2 copy.74
  67.1 0.3 copy.56
  67.4 1.3 all-gather.2.cloned.1.call-done
  68.8 52.6 %while.16 = (s32[]{:T(128)}, f32[2,8,256]{2,1,0:T(8,128)S(1)}, f32[2,8,256]{2,1,0:T(8,128)S(1)}, f32[256,2,8,128]{0,3,2,1:T(8,128)}, s32[256]{0:T(256)S(1)}, /*i...) while((s32[]{:T(128)}, f32[2,8,256]{2,1,0:T(8,128)S(1)}, ...), condition=%wide.region_6.7_spmd.clone.clone, body=%wide.region_2.6_spmd.clone.clone.sunk | while | flops 2204406784 | bytes 131365624 | solution.py:84
  68.8 0.6 dynamic_slice.17
  69.3 0.6 subtract_multiply_fusion.2
  70.2 0.1 convert_reduce_fusion.3
  70.2 0.3 compare_and_fusion.2
  70.6 1.3 copy_bitcast_fusion.2
  71.9 0.1 fusion.32
  72.0 0.1 squeeze.23
  72.1 7.2 %fusion.33 = (f32[2,8,256]{2,1,0:T(8,128)S(1)}, f32[2,1024,256,8]{2,1,3,0:T(8,128)}) fusion(pred[256,1024]{0,1:T(8,128)(4,1)S(1)} %compare_and_fusion.2, bf16[256,2,8,128]{3,0,2,1:T(8,128)(2,1)S(1)} %get-tuple-element.319, bf16[1024,2,128,1]{2,1,0,3:T(2,128)(2,1)S(1)} %bitcast.83), kind=kOutput, calls=%fused_computation.3.clone.1 | convolution fusion | flops 1086320640 | bytes 18628608 | tf_op jit(solution)/shard_map/while/body/eval_jaxpr/rgjd,kgd->gjrk/dot_general | solution.py:64
  79.3 0.1 reshape.206
  79.4 9.7 %bitcast_add_fusion.2 = f32[256,2,8,128]{0,3,2,1:T(8,128)} fusion(f32[256,2,8,128]{0,3,2,1:T(8,128)} %get-tuple-element.301, f32[2,1024,256,8]{2,1,3,0:T(8,128)} %get-tuple-element.283, f32[2,8,256]{2,1,0:T(8,128)S(1)} %get-tuple-element.311, pred[256,1024]{0,1:T(8,128)(4,1)S(1)} %compare_and_fusion.2, f32[256,2,8]{0,2,1:T(8,128)S(1)} %get-tuple-element.284, ...), kind=kOutput, calls=%fused_computation.8.clone.1 | convolution fusion | flops 1096286208 | bytes 21790720 | tf_op jit(solution)/shard_map/while/body/eval_jaxpr/gjrk,kgd->rgjd/dot_general | solution.py:74
  89.1 1.6 %copy-done = f32[2,1024,256,8]{2,1,3,0:T(8,128)S(1)} copy-done((f32[2,1024,256,8]{2,1,3,0:T(8,128)S(1)}, f32[2,1024,256,8]{2,1,3,0:T(8,128)}, u32[]{:S(2)}) %copy-start) | copy-done | bytes 16777240 | tf_op jit(solution)/shard_map/while
  90.7 4.0 %fusion.35 = f32[2,8,256]{2,1,0:T(8,128)S(1)} fusion(f32[2,1024,256,8]{2,1,3,0:T(8,128)S(1)} %copy-done, f32[2,8,256]{2,1,0:T(8,128)S(1)} %get-tuple-element.311, pred[256,1024]{0,1:T(8,128)(4,1)S(1)} %compare_and_fusion.2), kind=kLoop, calls=%fused_computation.5.clone.1 | loop fusion | flops 20967424 | bytes 17072128 | tf_op jit(solution)/shard_map/while/body/eval_jaxpr/reduce_sum | solution.py:73
  94.8 0.6 dynamic_slice.17
  95.4 0.6 subtract_multiply_fusion.2
  96.2 0.1 convert_reduce_fusion.3
  96.3 0.3 compare_and_fusion.2
  96.6 1.3 copy_bitcast_fusion.2
  97.9 0.1 fusion.32
  98.0 0.1 squeeze.23
  98.1 7.2 %fusion.33 = (f32[2,8,256]{2,1,0:T(8,128)S(1)}, f32[2,1024,256,8]{2,1,3,0:T(8,128)}) fusion(pred[256,1024]{0,1:T(8,128)(4,1)S(1)} %compare_and_fusion.2, bf16[256,2,8,128]{3,0,2,1:T(8,128)(2,1)S(1)} %get-tuple-element.319, bf16[1024,2,128,1]{2,1,0,3:T(2,128)(2,1)S(1)} %bitcast.83), kind=kOutput, calls=%fused_computation.3.clone.1 | convolution fusion | flops 1086320640 | bytes 18628608 | tf_op jit(solution)/shard_map/while/body/eval_jaxpr/rgjd,kgd->gjrk/dot_general | solution.py:64
  105.3 0.1 reshape.206
  105.5 10.3 %bitcast_add_fusion.2 = f32[256,2,8,128]{0,3,2,1:T(8,128)} fusion(f32[256,2,8,128]{0,3,2,1:T(8,128)} %get-tuple-element.301, f32[2,1024,256,8]{2,1,3,0:T(8,128)} %get-tuple-element.283, f32[2,8,256]{2,1,0:T(8,128)S(1)} %get-tuple-element.311, pred[256,1024]{0,1:T(8,128)(4,1)S(1)} %compare_and_fusion.2, f32[256,2,8]{0,2,1:T(8,128)S(1)} %get-tuple-element.284, ...), kind=kOutput, calls=%fused_computation.8.clone.1 | convolution fusion | flops 1096286208 | bytes 21790720 | tf_op jit(solution)/shard_map/while/body/eval_jaxpr/gjrk,kgd->rgjd/dot_general | solution.py:74
  115.8 1.6 %copy-done = f32[2,1024,256,8]{2,1,3,0:T(8,128)S(1)} copy-done((f32[2,1024,256,8]{2,1,3,0:T(8,128)S(1)}, f32[2,1024,256,8]{2,1,3,0:T(8,128)}, u32[]{:S(2)}) %copy-start) | copy-done | bytes 16777240 | tf_op jit(solution)/shard_map/while
  117.4 4.0 %fusion.35 = f32[2,8,256]{2,1,0:T(8,128)S(1)} fusion(f32[2,1024,256,8]{2,1,3,0:T(8,128)S(1)} %copy-done, f32[2,8,256]{2,1,0:T(8,128)S(1)} %get-tuple-element.311, pred[256,1024]{0,1:T(8,128)(4,1)S(1)} %compare_and_fusion.2), kind=kLoop, calls=%fused_computation.5.clone.1 | loop fusion | flops 20967424 | bytes 17072128 | tf_op jit(solution)/shard_map/while/body/eval_jaxpr/reduce_sum | solution.py:73
  121.4 1.8 %divide_convert_fusion = bf16[256,2,8,128]{0,3,2,1:T(8,128)(2,1)S(1)} fusion(f32[256,2,8,128]{0,3,2,1:T(8,128)} %get-tuple-element.66, f32[256,2,8]{0,2,1:T(8,128)S(1)} %bitcast.97), kind=kLoop, calls=%fused_computation.31 | loop fusion | flops 1048576 | bytes 3162112 | tf_op jit(solution)/shard_map/convert_element_type | solution.py:86
  123.2 0.3 reshape.199
  123.5 3.1 %copy.58 = bf16[1,2,128,2048]{3,1,0,2:T(2,128)(2,1)S(1)} copy(bf16[1,2,128,2048]{2,1,3,0:T(2,128)(2,1)S(1)} %reshape.199) | data formatting | bytes 2097152 | tf_op jit(solution)/shard_map/reshape | solution.py:87
  126.6 18.5 %all_to_all.49 = bf16[1,2,128,2048]{3,1,0,2:T(2,128)(2,1)S(1)} all-to-all(bf16[1,2,128,2048]{3,1,0,2:T(2,128)(2,1)S(1)} %copy.58), channel_id=1, replica_groups=mesh['ctx'=8,'head'=4] {'head'}, dimensions={2} | all-to-all | bytes 2097152 | tf_op jit(solution)/shard_map/all_to_all | solution.py:88
  145.1 0.3 copy.59
  145.4 1.0 copy.73
  (25 shorter events, 0.4 us)
Async XLA Ops:
  6.5 34.3 %copy-start.1 = (s32[4]{0:T(128)S(1)}, s32[4]{0:T(128)}, u32[]{:S(2)}) copy-start(s32[4]{0:T(128)} %param.7) | copy-start | bytes 52
  6.5 62.2 %all-gather.2.cloned.1.call-start = ((), (), s32[]{:S(2)}) async-start(), calls=%async_computation.3 | async-start | bytes 2359296 | tf_op jit(solution)/shard_map/all_gather | solution.py:43
  36.3 18.1 %all-to-all-start.1 = ((bf16[4,2,65536]{2,1,0:T(2,128)(2,1)}), bf16[4,2,65536]{2,1,0:T(2,128)(2,1)S(1)}, u32[]{:S(2)}, u32[]{:S(2)}) async-start(bf16[4,2,65536]{2,1,0:T(2,128)(2,1)} %reshape.203), calls=%async_computation.1 | async-start | bytes 2097152 | tf_op jit(solution)/shard_map/all_to_all | solution.py:23
  79.4 11.3 %copy-start = (f32[2,1024,256,8]{2,1,3,0:T(8,128)S(1)}, f32[2,1024,256,8]{2,1,3,0:T(8,128)}, u32[]{:S(2)}) copy-start(f32[2,1024,256,8]{2,1,3,0:T(8,128)} %get-tuple-element.283) | copy-start | bytes 50331652 | tf_op jit(solution)/shard_map/while
  105.5 11.9 %copy-start = (f32[2,1024,256,8]{2,1,3,0:T(8,128)S(1)}, f32[2,1024,256,8]{2,1,3,0:T(8,128)}, u32[]{:S(2)}) copy-start(f32[2,1024,256,8]{2,1,3,0:T(8,128)} %get-tuple-element.283) | copy-start | bytes 50331652 | tf_op jit(solution)/shard_map/while
Sparse Core Ops, SparseCore 0:
  20.8 47.8 all-gather.1
where the time goes:
time: 156 us; the launch traced here: 153 us
  local copies, waits for them, and re-layouts  46.1 us (30%)
  matrix products  34.3 us (22%)
  blocking collectives  27.6 us (18%)
  waiting for transfers between devices  14.6 us (9%)
  between operations  13.5 us (9%)
  other arithmetic  12.5 us (8%)
  starting transfers between devices  4.49 us (3%)
    unnamed x10, local copies, waits for them, and re-layouts  23.3 us
    dot_general x2, matrix products, advance(): jnp.einsum('gjrk,kgd->rgjd', probs.astype(jnp.bfloat16), value_rows, pref...  20 us
    all_to_all x1, blocking collectives, local(): lax.all_to_all(result, 'head', split_axis=2, concat_axis=3, tiled=True)  18.5 us
    dot_general x2, matrix products, advance(): jnp.einsum('rgjd,kgd->gjrk', query_rows, key_row_block, preferred_element...  14.3 us
    all_to_all x1, waiting for transfers between devices, local(): lax.all_to_all(query, 'head', split_axis=3, concat_axis=2, tiled=True)  13.3 us
    all_to_all x1, blocking collectives, local(): lax.all_to_all(stacked, 'head', split_axis=3, concat_axis=2, tiled=True)  9.05 us
    all_to_all x1, local copies, waits for them, and re-layouts, local(): lax.all_to_all(query, 'head', split_axis=3, concat_axis=2, tiled=True)  8.96 us
    reduce_sum x2, other arithmetic, advance(): totals = totals * rescale + jnp.sum(probs, axis=-1)  7.97 us
  transfers between devices with their start and end apart: 2, of which 2 were waited for; matrix products, arithmetic and copies ran while one was open for 19% of the time, Pallas kernels for 0%

commit v1 on v0

v1 whole, which is shorter than its diff:
```python
import functools
import math

import jax
import jax.numpy as jnp
from jax import lax
from jax.experimental import pallas as pl
from jax.experimental.pallas import tpu as pltpu
from jax.sharding import PartitionSpec as P

QUERY_HEADS = 64
KEY_VALUE_HEADS = 8
HEAD_WIDTH = 128
BLK = 128
MESH = pl.DeviceIdType.MESH
LOW = -1e30


def ring_place(c, n):
    return jnp.where(c % 2 == 0, c // 2, n - 1 - c // 2)


def ring_member(p, n):
    return jnp.where(p < n // 2, 2 * p, 2 * (n - 1 - p) + 1)


def gather_kernel(n, heads, q_ref, kv_ref, qo_ref, kvo_ref, q_own, kv_own,
                  local_sem, q_send, q_recv, kv_send, kv_recv, ring_send, ring_recv):
    me_c, me_h = lax.axis_index("ctx"), lax.axis_index("head")
    tokens = q_ref.shape[2]
    q_width, kv_width = qo_ref.shape[2], kvo_ref.shape[3]
    place = ring_place(me_c, n)
    right = ring_member((place + 1) % n, n)
    left = ring_member((place + n - 1) % n, n)

    own_q = pltpu.make_async_copy(
        q_ref.at[0, :, :, pl.ds(pl.multiple_of(me_h * q_width, q_width), q_width)], q_own, local_sem.at[0])
    own_kv = pltpu.make_async_copy(
        kv_ref.at[0, :, :, :, pl.ds(pl.multiple_of(me_h * kv_width, kv_width), kv_width)], kv_own, local_sem.at[1])
    own_kv.start()
    own_q.start()

    barrier = pltpu.get_barrier_semaphore()
    for d in range(1, heads):
        pl.semaphore_signal(barrier, inc=1, device_id={"head": (me_h + d) % heads}, device_id_type=MESH)
    for c in (left, right):
        pl.semaphore_signal(barrier, inc=1, device_id={"ctx": c}, device_id_type=MESH)
    pl.semaphore_wait(barrier, heads - 1 + 2)

    row0 = pl.multiple_of(me_h * tokens, tokens)
    blocks = (me_c, 2 * n - 1 - me_c)
    kv_copies, q_copies = [], []
    for d in range(1, heads):
        peer = (me_h + d) % heads
        for h in range(2):
            copy = pltpu.make_async_remote_copy(
                src_ref=kv_ref.at[0, :, h, :, pl.ds(pl.multiple_of(peer * kv_width, kv_width), kv_width)],
                dst_ref=kvo_ref.at[:, blocks[h], pl.ds(row0, tokens), :],
                send_sem=kv_send.at[d - 1, h], recv_sem=kv_recv.at[d - 1, h],
                device_id={"head": peer}, device_id_type=MESH)
            copy.start()
            kv_copies.append(copy)
    for d in range(1, heads):
        peer = (me_h + d) % heads
        copy = pltpu.make_async_remote_copy(
            src_ref=q_ref.at[0, :, :, pl.ds(pl.multiple_of(peer * q_width, q_width), q_width)],
            dst_ref=qo_ref.at[:, pl.ds(row0, tokens), :],
            send_sem=q_send.at[d - 1], recv_sem=q_recv.at[d - 1],
            device_id={"head": peer}, device_id_type=MESH)
        copy.start()
        q_copies.append(copy)

    own_kv.wait()
    puts = []
    for h in range(2):
        put = pltpu.make_async_copy(kv_own.at[:, h], kvo_ref.at[:, blocks[h], pl.ds(row0, tokens), :],
                                    local_sem.at[2 + h])
        put.start()
        puts.append(put)
    own_q.wait()
    put_q = pltpu.make_async_copy(q_own, qo_ref.at[:, pl.ds(row0, tokens), :], local_sem.at[4])
    put_q.start()
    for put in puts:
        put.wait()
    for copy in kv_copies:
        copy.wait_recv()

    def hop(step, a, h):
        origin = ring_member((place + n - step) % n if a == 0 else (place + step) % n, n)
        block = origin if h == 0 else 2 * n - 1 - origin
        return pltpu.make_async_remote_copy(
            src_ref=kvo_ref.at[a, block], dst_ref=kvo_ref.at[a, block],
            send_sem=ring_send.at[step, a, h], recv_sem=ring_recv.at[step, a, h],
            device_id={"ctx": right if a == 0 else left}, device_id_type=MESH)

    hops = []
    for step in range(n - 1):
        now = []
        for h in range(2):
            for a in range(2):
                if step > 0:
                    hops[step - 1][2 * h + a].wait_recv()
                copy = hop(step, a, h)
                copy.start()
                now.append(copy)
        hops.append(now)
    for copy in hops[-1]:
        copy.wait_recv()
    for now in hops:
        for copy in now:
            copy.wait_send()
    for copy in kv_copies:
        copy.wait_send()
    put_q.wait()
    for copy in q_copies:
        copy.wait_recv()
        copy.wait_send()


def attend_kernel(n, groups, per_group, docs_ref, where_ref, q_ref, kv_ref, o_ref, m_ref, l_ref, acc_ref):
    half = pl.program_id(0)
    span = q_ref.shape[1]
    c = where_ref[0]
    block = jnp.where(half == 0, c, 2 * n - 1 - c)
    first = jnp.int32(0)
    end = jnp.int32(0)
    for j in range(docs_ref.shape[0]):
        end = end + docs_ref[j]
        first = jnp.where(end <= block, end, first)
    factor = HEAD_WIDTH ** -0.5 * math.log2(math.e)
    pair = 2
    rows = pair * span
    lanes = HEAD_WIDTH

    for g in range(groups):
        def queries(t):
            base = (g * per_group + t * pair) * HEAD_WIDTH
            return jnp.concatenate(
                [q_ref[0, :, base + j * HEAD_WIDTH: base + (j + 1) * HEAD_WIDTH] for j in range(pair)], axis=0)

        def keyval(a, at, count):
            out = kv_ref[a, pl.ds(at, count), :, g * HEAD_WIDTH:(g + 1) * HEAD_WIDTH]
            return out.reshape(count * span, HEAD_WIDTH)

        def scores_of(t, keys):
            return lax.dot_general(queries(t), keys, (((1,), (1,)), ((), ())),
                                   preferred_element_type=jnp.float32)

        def lane_sums(p):
            total = p[:, :lanes]
            for i in range(1, p.shape[1] // lanes):
                total = total + p[:, i * lanes:(i + 1) * lanes]
            return total

        def mix(p, values):
            return lax.dot_general(p.astype(jnp.bfloat16), values, (((1,), (0,)), ((), ())),
                                   preferred_element_type=jnp.float32)

        tiles = per_group // pair
        keys, values = keyval(0, block, 1), keyval(1, block, 1)
        row_at = lax.broadcasted_iota(jnp.int32, (rows, span), 0) % span
        seen = lax.broadcasted_iota(jnp.int32, (rows, span), 1) <= row_at
        for t in range(tiles):
            s = jnp.where(seen, scores_of(t, keys), LOW)
            m = jnp.max(s, axis=-1, keepdims=True)
            p = jnp.exp2((s - m) * factor)
            m_ref[t] = jnp.broadcast_to(m, (rows, lanes))
            l_ref[t] = lane_sums(p)
            acc_ref[t] = mix(p, values)

        def fold(at, count):
            keys, values = keyval(0, at, count), keyval(1, at, count)
            for t in range(tiles):
                s = scores_of(t, keys)
                m_old = m_ref[t]
                m = jnp.maximum(m_old, jnp.max(s, axis=-1, keepdims=True))
                p = jnp.exp2((s - jnp.tile(m, (1, count * span // lanes))) * factor)
                alpha = jnp.exp2((m_old - m) * factor)
                m_ref[t] = m
                l_ref[t] = l_ref[t] * alpha + lane_sums(p)
                acc_ref[t] = acc_ref[t] * alpha + mix(p, values)

        inner = block - first

        def body(i, carry):
            fold(first + 2 * i, 2)
            return carry

        lax.fori_loop(0, inner // 2, body, 0)

        @pl.when(inner % 2 == 1)
        def _():
            fold(block - 1, 1)

        for t in range(tiles):
            out = acc_ref[t] / jnp.sum(l_ref[t], axis=-1, keepdims=True)
            out = out.astype(o_ref.dtype)
            for j in range(pair):
                base = (g * per_group + t * pair + j) * HEAD_WIDTH
                o_ref[0, :, base:base + HEAD_WIDTH] = out[j * span:(j + 1) * span]


def return_kernel(heads, o_ref, out_ref, own, local_sem, send, recv):
    me_h = lax.axis_index("head")
    tokens, width = out_ref.shape[2], o_ref.shape[2]
    take = pltpu.make_async_copy(
        o_ref.at[:, pl.ds(pl.multiple_of(me_h * tokens, tokens), tokens), :], own, local_sem.at[0])
    take.start()
    barrier = pltpu.get_barrier_semaphore()
    for d in range(1, heads):
        pl.semaphore_signal(barrier, inc=1, device_id={"head": (me_h + d) % heads}, device_id_type=MESH)
    pl.semaphore_wait(barrier, heads - 1)
    place = out_ref.at[0, :, :, pl.ds(pl.multiple_of(me_h * width, width), width)]
    copies = []
    for d in range(1, heads):
        peer = (me_h + d) % heads
        copy = pltpu.make_async_remote_copy(
            src_ref=o_ref.at[:, pl.ds(pl.multiple_of(peer * tokens, tokens), tokens), :], dst_ref=place,
            send_sem=send.at[d - 1], recv_sem=recv.at[d - 1],
            device_id={"head": peer}, device_id_type=MESH)
        copy.start()
        copies.append(copy)
    take.wait()
    put = pltpu.make_async_copy(own, place, local_sem.at[1])
    put.start()
    put.wait()
    for copy in copies:
        copy.wait()


def local(query, keyval, doc_blocks):
    n, heads = lax.axis_size("ctx"), lax.axis_size("head")
    tokens = query.shape[2]
    span = tokens * heads
    assert span == BLK
    q_width, kv_width = query.shape[3] // heads, keyval.shape[4] // heads
    groups, per_group = kv_width // HEAD_WIDTH, QUERY_HEADS // KEY_VALUE_HEADS
    kind = query.dtype
    anywhere = pl.BlockSpec(memory_space=pl.ANY)
    dma = pltpu.SemaphoreType.DMA
    rows, kv = pl.pallas_call(
        functools.partial(gather_kernel, n, heads),
        out_shape=(jax.ShapeDtypeStruct((2, span, q_width), kind),
                   jax.ShapeDtypeStruct((2, 2 * n, span, kv_width), kind)),
        in_specs=[anywhere, anywhere],
        out_specs=(anywhere, anywhere),
        scratch_shapes=[
            pltpu.VMEM((2, tokens, q_width), kind),
            pltpu.VMEM((2, 2, tokens, kv_width), kind),
            dma((5,)), dma((heads - 1,)), dma((heads - 1,)),
            dma((heads - 1, 2)), dma((heads - 1, 2)),
            dma((n - 1, 2, 2)), dma((n - 1, 2, 2)),
        ],
        compiler_params=pltpu.CompilerParams(collective_id=0, has_side_effects=True),
        name="gather",
    )(query, keyval)

    mine = jnp.reshape(lax.axis_index("ctx"), (1,)).astype(jnp.int32)
    pair_rows = 2 * span
    tiles = per_group // 2
    state = pltpu.VMEM((tiles, pair_rows, HEAD_WIDTH), jnp.float32)
    mixed = pl.pallas_call(
        functools.partial(attend_kernel, n, groups, per_group),
        out_shape=jax.ShapeDtypeStruct((2, span, q_width), kind),
        grid_spec=pltpu.PrefetchScalarGridSpec(
            num_scalar_prefetch=2, grid=(2,),
            in_specs=[pl.BlockSpec((1, span, q_width), lambda h, *_: (h, 0, 0)),
                      pl.BlockSpec((2, 2 * n, span, kv_width), lambda h, *_: (0, 0, 0, 0),
                                   pipeline_mode=pl.Buffered(1))],
            out_specs=pl.BlockSpec((1, span, q_width), lambda h, *_: (h, 0, 0)),
            scratch_shapes=[state, state, state]),
        name="attend",
    )(doc_blocks, mine, rows, kv)

    return pl.pallas_call(
        functools.partial(return_kernel, heads),
        out_shape=jax.ShapeDtypeStruct(query.shape, kind),
        in_specs=[anywhere],
        out_specs=anywhere,
        scratch_shapes=[pltpu.VMEM((2, tokens, q_width), kind), dma((2,)), dma((heads - 1,)), dma((heads - 1,))],
        compiler_params=pltpu.CompilerParams(collective_id=1, has_side_effects=True),
        name="return",
    )(mixed)


def solution(mesh):
    placed = (P("ctx", None, "head", None), P("ctx", None, None, "head", None), P())
    return jax.shard_map(
        local, mesh=mesh, in_specs=placed, out_specs=P("ctx", None, "head", None), check_vma=False
    )
```

time: 156 us -> 69.9 us (0.45)
  the two profiles are of different devices: /device:TPU:1 before, /device:TPU:13 now
where the time goes in v1:
time: 69.9 us; the launch traced here: 69.7 us
  Pallas kernels  67.4 us (96%)
  local copies, waits for them, and re-layouts  2.26 us (3%)
    pallas_call x1, Pallas kernels, local(): pl.pallas_call(functools.partial(gather_kernel, n, heads), out_shape=(jax...  33.3 us
    pallas_call x1, Pallas kernels, local(): pl.pallas_call(functools.partial(return_kernel, heads), out_shape=jax.Sha...  17.8 us
    pallas_call x1, Pallas kernels, local(): pl.pallas_call(functools.partial(attend_kernel, n, groups, per_group), ou...  16.3 us
    unnamed x1, local copies, waits for them, and re-layouts  2.26 us

profile of v1, /device:TPU:13, one launch (start us, length us, event | category | flops | bytes accessed | tf_op | source)
XLA Modules:
  0.0 69.7 jit_solution(4562646726432288893)
XLA Ops:
  0.0 33.3 %gather.1 = (bf16[2,128,2048]{2,1,0:T(8,128)(2,1)}, bf16[2,16,128,256]{3,2,1,0:T(8,128)(2,1)}) custom-call(bf16[1,2,32,8192]{3,2,1,0:T(8,128)(2,1)} %q_ref.1, bf16[1,2,2,32,1024]{4,3,2,1,0:T(8,128)(2,1)} %kv_ref.1), custom_call_target="tpu_custom_call" | custom-call | tf_op jit(solution)/shard_map/gather/pallas_call | solution.py:241
  33.3 16.3 %attend.1.o_ref = bf16[2,128,2048]{2,1,0:T(8,128)(2,1)} custom-call(s32[4]{0:T(128)} %docs_ref.1, s32[1]{0:T(128)} %bitcast.where_ref, bf16[2,128,2048]{2,1,0:T(8,128)(2,1)} %get-tuple-element.7.q_ref, bf16[2,16,128,256]{3,2,1,0:T(8,128)(2,1)} %get-tuple-element.8.kv_ref), custom_call_target="tpu_custom_call" | custom-call | tf_op jit(solution)/shard_map/attend/pallas_call | solution.py:262
  49.6 17.8 %return.1 = bf16[1,2,32,8192]{3,2,1,0:T(8,128)(2,1)} custom-call(bf16[2,128,2048]{2,1,0:T(8,128)(2,1)} %attend.1.o_ref), custom_call_target="tpu_custom_call" | custom-call | tf_op jit(solution)/shard_map/return/pallas_call | solution.py:275
  67.4 2.3 %copy.5 = bf16[1,2,32,8192]{3,2,1,0:T(8,128)(2,1)} copy(bf16[1,2,32,8192]{3,2,1,0:T(8,128)(2,1)} %return.1) | data formatting | bytes 2097152

commit v2 on v0

v2 whole, which is shorter than its diff:
```python
import functools
import math

import jax
import jax.numpy as jnp
from jax import lax
from jax.experimental import pallas as pl
from jax.experimental.pallas import tpu as pltpu
from jax.sharding import PartitionSpec as P

QUERY_HEADS = 64
KEY_VALUE_HEADS = 8
HEAD_WIDTH = 128
BLK = 128
MESH = pl.DeviceIdType.MESH
LOW = -1e30


def ring_place(c, n):
    return jnp.where(c % 2 == 0, c // 2, n - 1 - c // 2)


def ring_member(p, n):
    return jnp.where(p < n // 2, 2 * p, 2 * (n - 1 - p) + 1)


def fused_kernel(n, heads, per_group, docs_ref, q_ref, kv_ref, out_ref, qbuf, kvbuf, obuf, m_ref, l_ref, acc_ref,
                 own_sem, q_send, q_recv, kv_send, kv_recv, ring_send, ring_recv, o_send, o_recv):
    me_c, me_h = lax.axis_index("ctx"), lax.axis_index("head")
    tokens, half = q_ref.shape[2], n // 2
    groups, span, width = qbuf.shape[0], qbuf.shape[2], qbuf.shape[3]
    place = ring_place(me_c, n)
    right = ring_member((place + 1) % n, n)
    left = ring_member((place + n - 1) % n, n)
    mine = (me_c, 2 * n - 1 - me_c)
    row0 = pl.multiple_of(me_h * tokens, tokens)

    def q_part(peer, g):
        at = pl.multiple_of((peer * groups + g) * width, width)
        return q_ref.at[0, :, :, pl.ds(at, width)]

    def kv_part(peer, g, h):
        at = pl.multiple_of((peer * groups + g) * HEAD_WIDTH, HEAD_WIDTH)
        return kv_ref.at[0, :, h, :, pl.ds(at, HEAD_WIDTH)]

    own = []
    for g in range(groups):
        for h in range(2):
            own.append(pltpu.make_async_copy(
                kv_part(me_h, g, h), kvbuf.at[g, mine[h], :, pl.ds(row0, tokens), :], own_sem.at[3 * g + h]))
        own.append(pltpu.make_async_copy(
            q_part(me_h, g), qbuf.at[g, :, pl.ds(row0, tokens), :], own_sem.at[3 * g + 2]))
    for copy in own:
        copy.start()

    barrier = pltpu.get_barrier_semaphore()
    for d in range(1, heads):
        pl.semaphore_signal(barrier, inc=1, device_id={"head": (me_h + d) % heads}, device_id_type=MESH)
    for c in (left, right):
        pl.semaphore_signal(barrier, inc=1, device_id={"ctx": c}, device_id_type=MESH)
    pl.semaphore_wait(barrier, heads - 1 + 2)

    kv_copies = [[] for _ in range(groups)]
    q_copies = [[] for _ in range(groups)]
    for g in range(groups):
        for d in range(1, heads):
            peer = (me_h + d) % heads
            for h in range(2):
                copy = pltpu.make_async_remote_copy(
                    src_ref=kv_part(peer, g, h), dst_ref=kvbuf.at[g, mine[h], :, pl.ds(row0, tokens), :],
                    send_sem=kv_send.at[g, d - 1, h], recv_sem=kv_recv.at[g, d - 1, h],
                    device_id={"head": peer}, device_id_type=MESH)
                copy.start()
                kv_copies[g].append(copy)
    for g in range(groups):
        for d in range(1, heads):
            peer = (me_h + d) % heads
            copy = pltpu.make_async_remote_copy(
                src_ref=q_part(peer, g), dst_ref=qbuf.at[g, :, pl.ds(row0, tokens), :],
                send_sem=q_send.at[g, d - 1], recv_sem=q_recv.at[g, d - 1],
                device_id={"head": peer}, device_id_type=MESH)
            copy.start()
            q_copies[g].append(copy)

    def member_at(d, distance):
        return ring_member((place + n - distance) % n if d == 0 else (place + distance) % n, n)

    def hop(g, d, t, h):
        origin = member_at(d, t)
        block = origin if h == 0 else 2 * n - 1 - origin
        return pltpu.make_async_remote_copy(
            src_ref=kvbuf.at[g, block], dst_ref=kvbuf.at[g, block],
            send_sem=ring_send.at[g, d, t, h], recv_sem=ring_recv.at[g, d, t, h],
            device_id={"ctx": right if d == 0 else left}, device_id_type=MESH)

    def arrived(g, d, t):
        for h in range(2):
            hop(g, d, t, h).wait_recv()

    def forward(g, d, t):
        for h in range(2):
            hop(g, d, t - 1, h).wait_recv()
            hop(g, d, t, h).start()

    factor = HEAD_WIDTH ** -0.5 * math.log2(math.e)
    pair = 2
    tiles, rows = per_group // pair, pair * span

    def doc_of(block):
        end, found = jnp.int32(0), jnp.int32(0)
        for j in range(docs_ref.shape[0]):
            end = end + docs_ref[j]
            found = found + jnp.where(end <= block, 1, 0).astype(jnp.int32)
        return found

    def scores_of(g, hq, t, keys):
        base = t * pair * HEAD_WIDTH
        queries = jnp.concatenate(
            [qbuf[g, hq, :, base + j * HEAD_WIDTH: base + (j + 1) * HEAD_WIDTH] for j in range(pair)], axis=0)
        return lax.dot_general(queries, keys, (((1,), (1,)), ((), ())), preferred_element_type=jnp.float32)

    def mix(p, values):
        return lax.dot_general(p.astype(jnp.bfloat16), values, (((1,), (0,)), ((), ())),
                               preferred_element_type=jnp.float32)

    def fold(g, hq, block):
        same = doc_of(block) == doc_of(jnp.where(hq == 0, mine[0], mine[1]))
        shift = jnp.where(same, jnp.float32(0), jnp.float32(-LOW))
        keys, values = kvbuf[g, block, 0], kvbuf[g, block, 1]
        for t in range(tiles):
            s = scores_of(g, hq, t, keys)
            m_old = m_ref[hq, t]
            m = jnp.maximum(m_old, jnp.max(s, axis=-1, keepdims=True) - shift)
            p = jnp.exp2((s - (m + shift)) * factor)
            alpha = jnp.exp2((m_old - m) * factor)
            m_ref[hq, t] = m
            l_ref[hq, t] = l_ref[hq, t] * alpha + p
            acc_ref[hq, t] = acc_ref[hq, t] * alpha + mix(p, values)

    def diagonal(g):
        def each(hq, carry):
            block = jnp.where(hq == 0, mine[0], mine[1])
            keys, values = kvbuf[g, block, 0], kvbuf[g, block, 1]
            row_at = lax.broadcasted_iota(jnp.int32, (rows, span), 0) % span
            seen = lax.broadcasted_iota(jnp.int32, (rows, span), 1) <= row_at
            for t in range(tiles):
                s = jnp.where(seen, scores_of(g, hq, t, keys), LOW)
                m = jnp.max(s, axis=-1, keepdims=True)
                p = jnp.exp2((s - m) * factor)
                m_ref[hq, t] = jnp.broadcast_to(m, (rows, span))
                l_ref[hq, t] = p
                acc_ref[hq, t] = mix(p, values)
            return carry

        lax.fori_loop(0, 2, each, 0)
        fold(g, 1, mine[0])

    def absorb(g, ways, t):
        def each(k, carry):
            if len(ways) == 2:
                distance = jnp.where(k < 2, n - 1 - t, t + 1)
            else:
                distance = n - 1 - t if ways[0] == 0 else t + 1
            origin = ring_member((place + distance) % n, n)
            lower = origin < me_c
            second = k % 2 == 1
            hq = jnp.where(second & lower, 0, 1)
            block = jnp.where(second & jnp.logical_not(lower), 2 * n - 1 - origin, origin)
            fold(g, hq, block)
            return carry

        lax.fori_loop(0, 2 * len(ways), each, 0)

    back = []

    def finish(g):
        def each(hq, carry):
            for t in range(tiles):
                out = acc_ref[hq, t] / jnp.sum(l_ref[hq, t], axis=-1, keepdims=True)
                out = out.astype(obuf.dtype)
                for j in range(pair):
                    base = (t * pair + j) * HEAD_WIDTH
                    obuf[g, hq, :, base:base + HEAD_WIDTH] = out[j * span:(j + 1) * span]
            return carry

        lax.fori_loop(0, 2, each, 0)
        place_out = out_ref.at[0, :, :, pl.ds(pl.multiple_of((me_h * groups + g) * width, width), width)]
        for d in range(1, heads):
            peer = (me_h + d) % heads
            copy = pltpu.make_async_remote_copy(
                src_ref=obuf.at[g, :, pl.ds(pl.multiple_of(peer * tokens, tokens), tokens), :], dst_ref=place_out,
                send_sem=o_send.at[g, d - 1], recv_sem=o_recv.at[g, d - 1],
                device_id={"head": peer}, device_id_type=MESH)
            copy.start()
            back.append(copy)
        copy = pltpu.make_async_copy(obuf.at[g, :, pl.ds(row0, tokens), :], place_out, own_sem.at[3 * groups + g])
        copy.start()
        back.append(copy)

    def ready(g):
        for h in range(2):
            own[3 * g + h].wait()
        for copy in kv_copies[g]:
            copy.wait_recv()
        for d in range(2):
            for h in range(2):
                hop(g, d, 0, h).start()

    def queries_ready(g):
        own[3 * g + 2].wait()
        for copy in q_copies[g]:
            copy.wait_recv()

    both, two = (0, 1), groups == 2
    for g in range(groups):
        ready(g)
    queries_ready(0)
    forward(0, 0, 1)
    forward(0, 1, 1)
    diagonal(0)
    absorb(0, both, 0)

    def early(t, carry):
        forward(0, 0, t)
        forward(0, 1, t)
        absorb(0, both, t - 1)
        return carry

    lax.fori_loop(2, half - 1, early, 0)
    forward(0, 0, half - 1)
    arrived(0, 1, half - 2)
    if two:
        forward(1, 1, 1)
    absorb(0, both, half - 2)
    if two:
        forward(1, 0, 1)
        forward(1, 1, 2)
    arrived(0, 0, half - 1)
    absorb(0, (0,), half - 1)
    finish(0)

    def late(t, carry):
        forward(1, 0, t)
        forward(1, 1, t + 1)
        absorb(1, both, t - 1)
        return carry

    if two:
        queries_ready(1)
        diagonal(1)
        absorb(1, both, 0)
        lax.fori_loop(2, half - 1, late, 0)
        arrived(1, 0, half - 2)
        absorb(1, both, half - 2)
        arrived(1, 1, half - 1)
        absorb(1, (1,), half - 1)
        finish(1)

    for g in range(groups):
        for copy in kv_copies[g] + q_copies[g]:
            copy.wait_send()
        for d in range(2):
            for t in range(half if d == g else half - 1):
                for h in range(2):
                    hop(g, d, t, h).wait_send()
    for copy in back:
        copy.wait()


def local(query, keyval, doc_blocks):
    n, heads = lax.axis_size("ctx"), lax.axis_size("head")
    tokens = query.shape[2]
    span = tokens * heads
    groups, per_group = keyval.shape[4] // heads // HEAD_WIDTH, QUERY_HEADS // KEY_VALUE_HEADS
    width = per_group * HEAD_WIDTH
    assert span == BLK and groups in (1, 2) and n % 2 == 0 and n >= 8
    kind = query.dtype
    anywhere = pl.BlockSpec(memory_space=pl.ANY)
    dma = pltpu.SemaphoreType.DMA
    state = pltpu.VMEM((2, per_group // 2, 2 * span, HEAD_WIDTH), jnp.float32)
    return pl.pallas_call(
        functools.partial(fused_kernel, n, heads, per_group),
        out_shape=jax.ShapeDtypeStruct(query.shape, kind),
        in_specs=[pl.BlockSpec(memory_space=pltpu.SMEM), anywhere, anywhere],
        out_specs=anywhere,
        scratch_shapes=[
            pltpu.VMEM((groups, 2, span, width), kind),
            pltpu.VMEM((groups, 2 * n, 2, span, HEAD_WIDTH), kind),
            pltpu.VMEM((groups, 2, span, width), kind),
            state, state, state,
            dma((4 * groups,)),
            dma((groups, heads - 1)), dma((groups, heads - 1)),
            dma((groups, heads - 1, 2)), dma((groups, heads - 1, 2)),
            dma((groups, 2, n // 2, 2)), dma((groups, 2, n // 2, 2)),
            dma((groups, heads - 1)), dma((groups, heads - 1)),
        ],
        compiler_params=pltpu.CompilerParams(collective_id=0, has_side_effects=True),
        name="fused",
    )(doc_blocks, query, keyval)


def solution(mesh):
    placed = (P("ctx", None, "head", None), P("ctx", None, None, "head", None), P())
    return jax.shard_map(
        local, mesh=mesh, in_specs=placed, out_specs=P("ctx", None, "head", None), check_vma=False
    )
```

time: 156 us -> 55.1 us (0.35); the launches traced: 153 us -> 55 us
  Pallas kernels: 0 us -> 52.7 us
  local copies, waits for them, and re-layouts: 46.1 us -> 2.26 us
  matrix products: 34.3 us -> 0 us
  blocking collectives: 27.6 us -> 0 us
  waiting for transfers between devices: 14.6 us -> 0 us
  between operations: 13.5 us -> 0.01 us
  other arithmetic: 12.5 us -> 0 us
  starting transfers between devices: 4.49 us -> 0 us
    pallas_call x0 -> x1, Pallas kernels: none -> 52.7 us  [local(): pl.pallas_call(functools.partial(fused_kernel, n, heads, per_group), out_...]
    dot_general x4 -> x0, matrix products: 34.3 us -> none  [the longest x2 20 us: advance(): jnp.einsum('gjrk,kgd->rgjd', probs.astype(jnp.bfloat16), value_rows, pref...]
    all_to_all x2 -> x0, blocking collectives: 27.6 us -> none  [the longest x1 18.5 us: local(): lax.all_to_all(result, 'head', split_axis=2, concat_axis=3, tiled=True)]
    unnamed x10 -> x1, local copies, waits for them, and re-layouts: 23.3 us -> 2.26 us
    all_to_all x1 -> x0, waiting for transfers between devices: 13.3 us -> none  [local(): lax.all_to_all(query, 'head', split_axis=3, concat_axis=2, tiled=True)]
    all_to_all x5 -> x0, local copies, waits for them, and re-layouts: 11.8 us -> none  [the longest x1 8.96 us: local(): lax.all_to_all(query, 'head', split_axis=3, concat_axis=2, tiled=True)]
    reduce_sum x5 -> x0, other arithmetic: 8.22 us -> none  [the longest x2 7.97 us: advance(): totals = totals * rescale + jnp.sum(probs, axis=-1)]
    all_to_all x1 -> x0, starting transfers between devices: 4.49 us -> none  [local(): lax.all_to_all(query, 'head', split_axis=3, concat_axis=2, tiled=True)]
  transfers between devices with their start and end apart: 2 -> 0, of which waited for: 2 -> 0; matrix products, arithmetic and copies ran while one was open for 19% -> 0% of each run, Pallas kernels for 0% -> 0%
where the time goes in v2:
time: 55.1 us; the launch traced here: 55 us
  Pallas kernels  52.7 us (96%)
  local copies, waits for them, and re-layouts  2.26 us (4%)
    pallas_call x1, Pallas kernels, local(): pl.pallas_call(functools.partial(fused_kernel, n, heads, per_group), out_...  52.7 us
    unnamed x1, local copies, waits for them, and re-layouts  2.26 us

profile of v2, /device:TPU:1, one launch (start us, length us, event | category | flops | bytes accessed | tf_op | source)
XLA Modules:
  0.0 55.0 jit_solution(1095134470449293147)
XLA Ops:
  0.0 52.7 %fused.1 = bf16[1,2,32,8192]{3,2,1,0:T(8,128)(2,1)} custom-call(s32[4]{0:T(128)} %docs_ref.1, bf16[1,2,32,8192]{3,2,1,0:T(8,128)(2,1)} %q_ref.1, bf16[1,2,2,32,1024]{4,3,2,1,0:T(8,128)(2,1)} %kv_ref.1), custom_call_target="tpu_custom_call" | custom-call | tf_op jit(solution)/shard_map/fused/pallas_call | solution.py:281
  52.7 2.3 %copy.5 = bf16[1,2,32,8192]{3,2,1,0:T(8,128)(2,1)} copy(bf16[1,2,32,8192]{3,2,1,0:T(8,128)(2,1)} %fused.1) | data formatting | bytes 2097152

commit v3 on v2

--- a/solution.py
+++ b/solution.py
@@ -123,18 +123,24 @@
         return lax.dot_general(p.astype(jnp.bfloat16), values, (((1,), (0,)), ((), ())),
                                preferred_element_type=jnp.float32)
 
-    def fold(g, hq, block):
-        same = doc_of(block) == doc_of(jnp.where(hq == 0, mine[0], mine[1]))
-        shift = jnp.where(same, jnp.float32(0), jnp.float32(-LOW))
-        keys, values = kvbuf[g, block, 0], kvbuf[g, block, 1]
+    def fold(g, hq, *blocks):
+        doc = doc_of(jnp.where(hq == 0, mine[0], mine[1]))
+        shifts = [jnp.where(doc_of(block) == doc, jnp.float32(0), jnp.float32(-LOW)) for block in blocks]
+        keys = jnp.concatenate([kvbuf[g, block, 0] for block in blocks], axis=0)
+        values = jnp.concatenate([kvbuf[g, block, 1] for block in blocks], axis=0)
         for t in range(tiles):
             s = scores_of(g, hq, t, keys)
             m_old = m_ref[hq, t]
-            m = jnp.maximum(m_old, jnp.max(s, axis=-1, keepdims=True) - shift)
-            p = jnp.exp2((s - (m + shift)) * factor)
+            parts = [s[:, i * span:(i + 1) * span] for i in range(len(blocks))]
+            top = parts[0] - shifts[0]
+            for part, shift in zip(parts[1:], shifts[1:]):
+                top = jnp.maximum(top, part - shift)
+            m = jnp.maximum(m_old, jnp.max(top, axis=-1, keepdims=True))
+            parts = [jnp.exp2((part - (m + shift)) * factor) for part, shift in zip(parts, shifts)]
+            p = jnp.concatenate(parts, axis=1)
             alpha = jnp.exp2((m_old - m) * factor)
             m_ref[hq, t] = m
-            l_ref[hq, t] = l_ref[hq, t] * alpha + p
+            l_ref[hq, t] = l_ref[hq, t] * alpha + sum(parts)
             acc_ref[hq, t] = acc_ref[hq, t] * alpha + mix(p, values)
 
     def diagonal(g):
@@ -156,46 +162,41 @@
         fold(g, 1, mine[0])
 
     def absorb(g, ways, t):
+        origins = [member_at(way, t + 1) for way in ways]
+        fold(g, 1, *origins)
+
         def each(k, carry):
-            if len(ways) == 2:
-                distance = jnp.where(k < 2, n - 1 - t, t + 1)
-            else:
-                distance = n - 1 - t if ways[0] == 0 else t + 1
-            origin = ring_member((place + distance) % n, n)
+            origin = jnp.where(k == 0, origins[0], origins[-1])
             lower = origin < me_c
-            second = k % 2 == 1
-            hq = jnp.where(second & lower, 0, 1)
-            block = jnp.where(second & jnp.logical_not(lower), 2 * n - 1 - origin, origin)
-            fold(g, hq, block)
+            fold(g, jnp.where(lower, 0, 1), jnp.where(lower, origin, 2 * n - 1 - origin))
             return carry
 
-        lax.fori_loop(0, 2 * len(ways), each, 0)
+        lax.fori_loop(0, len(ways), each, 0)
 
     back = []
 
     def finish(g):
-        def each(hq, carry):
+        cols = pl.ds(pl.multiple_of((me_h * groups + g) * width, width), width)
+        for hq in range(2):
             for t in range(tiles):
                 out = acc_ref[hq, t] / jnp.sum(l_ref[hq, t], axis=-1, keepdims=True)
                 out = out.astype(obuf.dtype)
                 for j in range(pair):
                     base = (t * pair + j) * HEAD_WIDTH
                     obuf[g, hq, :, base:base + HEAD_WIDTH] = out[j * span:(j + 1) * span]
-            return carry
-
-        lax.fori_loop(0, 2, each, 0)
-        place_out = out_ref.at[0, :, :, pl.ds(pl.multiple_of((me_h * groups + g) * width, width), width)]
-        for d in range(1, heads):
-            peer = (me_h + d) % heads
-            copy = pltpu.make_async_remote_copy(
-                src_ref=obuf.at[g, :, pl.ds(pl.multiple_of(peer * tokens, tokens), tokens), :], dst_ref=place_out,
-                send_sem=o_send.at[g, d - 1], recv_sem=o_recv.at[g, d - 1],
-                device_id={"head": peer}, device_id_type=MESH)
+            place_out = out_ref.at[0, hq, :, cols]
+            for d in range(1, heads):
+                peer = (me_h + d) % heads
+                copy = pltpu.make_async_remote_copy(
+                    src_ref=obuf.at[g, hq, pl.ds(pl.multiple_of(peer * tokens, tokens), tokens), :],
+                    dst_ref=place_out, send_sem=o_send.at[g, hq, d - 1], recv_sem=o_recv.at[g, hq, d - 1],
+                    device_id={"head": peer}, device_id_type=MESH)
+                copy.start()
+                back.append(copy)
+            copy = pltpu.make_async_copy(obuf.at[g, hq, pl.ds(row0, tokens), :], place_out,
+                                         own_sem.at[3 * groups + 2 * g + hq])
             copy.start()
             back.append(copy)
-        copy = pltpu.make_async_copy(obuf.at[g, :, pl.ds(row0, tokens), :], place_out, own_sem.at[3 * groups + g])
-        copy.start()
-        back.append(copy)
 
     def ready(g):
         for h in range(2):
@@ -214,42 +215,46 @@
     both, two = (0, 1), groups == 2
     for g in range(groups):
         ready(g)
-    queries_ready(0)
     forward(0, 0, 1)
     forward(0, 1, 1)
+    queries_ready(0)
     diagonal(0)
-    absorb(0, both, 0)
 
     def early(t, carry):
         forward(0, 0, t)
         forward(0, 1, t)
-        absorb(0, both, t - 1)
+        absorb(0, both, t - 2)
         return carry
 
     lax.fori_loop(2, half - 1, early, 0)
     forward(0, 0, half - 1)
-    arrived(0, 1, half - 2)
     if two:
         forward(1, 1, 1)
-    absorb(0, both, half - 2)
+    absorb(0, both, half - 3)
     if two:
         forward(1, 0, 1)
         forward(1, 1, 2)
+    arrived(0, 1, half - 2)
+    absorb(0, both, half - 2)
     arrived(0, 0, half - 1)
+    if two:
+        forward(1, 0, 2)
+        forward(1, 1, 3)
     absorb(0, (0,), half - 1)
     finish(0)
 
     def late(t, carry):
         forward(1, 0, t)
         forward(1, 1, t + 1)
-        absorb(1, both, t - 1)
+        absorb(1, both, t - 3)
         return carry
 
     if two:
         queries_ready(1)
         diagonal(1)
-        absorb(1, both, 0)
-        lax.fori_loop(2, half - 1, late, 0)
+        lax.fori_loop(3, half - 1, late, 0)
+        absorb(1, both, half - 4)
+        absorb(1, both, half - 3)
         arrived(1, 0, half - 2)
         absorb(1, both, half - 2)
         arrived(1, 1, half - 1)
@@ -288,11 +293,11 @@
             pltpu.VMEM((groups, 2 * n, 2, span, HEAD_WIDTH), kind),
             pltpu.VMEM((groups, 2, span, width), kind),
             state, state, state,
-            dma((4 * groups,)),
+            dma((5 * groups,)),
             dma((groups, heads - 1)), dma((groups, heads - 1)),
             dma((groups, heads - 1, 2)), dma((groups, heads - 1, 2)),
             dma((groups, 2, n // 2, 2)), dma((groups, 2, n // 2, 2)),
-            dma((groups, heads - 1)), dma((groups, heads - 1)),
+            dma((groups, 2, heads - 1)), dma((groups, 2, heads - 1)),
         ],
         compiler_params=pltpu.CompilerParams(collective_id=0, has_side_effects=True),
         name="fused",

time: 55.1 us -> 51.9 us (0.942)
  Pallas kernels: 52.7 us -> 49.4 us
    pallas_call x1, Pallas kernels: 52.7 us -> 49.4 us  [local(): pl.pallas_call(functools.partial(fused_kernel, n, heads, per_group), out_...]
where the time goes in v3:
time: 51.9 us; the launch traced here: 51.7 us
  Pallas kernels  49.4 us (95%)
  local copies, waits for them, and re-layouts  2.26 us (4%)
    pallas_call x1, Pallas kernels, local(): pl.pallas_call(functools.partial(fused_kernel, n, heads, per_group), out_...  49.4 us
    unnamed x1, local copies, waits for them, and re-layouts  2.26 us

profile of v3, /device:TPU:1, one launch (start us, length us, event | category | flops | bytes accessed | tf_op | source)
XLA Modules:
  0.0 51.7 jit_solution(7960084888422891706)
XLA Ops:
  0.0 49.4 %fused.1 = bf16[1,2,32,8192]{3,2,1,0:T(8,128)(2,1)} custom-call(s32[4]{0:T(128)} %docs_ref.1, bf16[1,2,32,8192]{3,2,1,0:T(8,128)(2,1)} %q_ref.1, bf16[1,2,2,32,1024]{4,3,2,1,0:T(8,128)(2,1)} %kv_ref.1), custom_call_target="tpu_custom_call" | custom-call | tf_op jit(solution)/shard_map/fused/pallas_call | solution.py:286
  49.4 2.3 %copy.5 = bf16[1,2,32,8192]{3,2,1,0:T(8,128)(2,1)} copy(bf16[1,2,32,8192]{3,2,1,0:T(8,128)(2,1)} %fused.1) | data formatting | bytes 2097152

commit v4 on v3

--- a/solution.py
+++ b/solution.py
@@ -103,7 +103,7 @@
             hop(g, d, t, h).start()
 
     factor = HEAD_WIDTH ** -0.5 * math.log2(math.e)
-    pair = 2
+    pair = 4
     tiles, rows = per_group // pair, pair * span
 
     def doc_of(block):
@@ -282,7 +282,7 @@
     kind = query.dtype
     anywhere = pl.BlockSpec(memory_space=pl.ANY)
     dma = pltpu.SemaphoreType.DMA
-    state = pltpu.VMEM((2, per_group // 2, 2 * span, HEAD_WIDTH), jnp.float32)
+    state = pltpu.VMEM((2, per_group // 4, 4 * span, HEAD_WIDTH), jnp.float32)
     return pl.pallas_call(
         functools.partial(fused_kernel, n, heads, per_group),
         out_shape=jax.ShapeDtypeStruct(query.shape, kind),

time: 51.9 us -> 51.4 us (level)
  no operation moved by 1% of the time
where the time goes in v4:
time: 51.4 us; the launch traced here: 51.2 us
  Pallas kernels  48.9 us (95%)
  local copies, waits for them, and re-layouts  2.26 us (4%)
    pallas_call x1, Pallas kernels, local(): pl.pallas_call(functools.partial(fused_kernel, n, heads, per_group), out_...  48.9 us
    unnamed x1, local copies, waits for them, and re-layouts  2.26 us

profile of v4, /device:TPU:1, one launch (start us, length us, event | category | flops | bytes accessed | tf_op | source)
XLA Modules:
  0.0 51.2 jit_solution(8013267967012898137)
XLA Ops:
  0.0 48.9 %fused.1 = bf16[1,2,32,8192]{3,2,1,0:T(8,128)(2,1)} custom-call(s32[4]{0:T(128)} %docs_ref.1, bf16[1,2,32,8192]{3,2,1,0:T(8,128)(2,1)} %q_ref.1, bf16[1,2,2,32,1024]{4,3,2,1,0:T(8,128)(2,1)} %kv_ref.1), custom_call_target="tpu_custom_call" | custom-call | tf_op jit(solution)/shard_map/fused/pallas_call | solution.py:286
  48.9 2.3 %copy.5 = bf16[1,2,32,8192]{3,2,1,0:T(8,128)(2,1)} copy(bf16[1,2,32,8192]{3,2,1,0:T(8,128)(2,1)} %fused.1) | data formatting | bytes 2097152
